TPU v7x, 512 devices: a whole 4x4x16 slice. The times are simulated.
512 devices in a mesh: section: 16 (over z), row: 8 (over y, core), col: 4 (over x).
Axes of the slice: x: 4, y: 4, z: 16, core: 2. Of those that a mesh axis runs over, the one named last changes fastest.
Arguments:
- x_fwd: bfloat16 [4096, 12288], P('section', 'row'), may hold values from -6 to 6
- dy_bwd: bfloat16 [4096, 12288], P(('section', 'row'), 'col'), may hold values from -6 to 6
- w_blocks: bfloat16 [16, 8, 4, 115, 128, 128], P('section', 'row', 'col'), may hold values from -0.09375 to 0.09375
- blk_row: int32 [16, 8, 4, 115], P('section', 'row', 'col'), may hold values from 0 to 11, as said below
- blk_col: int32 [16, 8, 4, 115], P('section', 'row', 'col'), may hold values from 0 to 23, as said below
- blk_count: int32 [16, 8, 4], P('section', 'row', 'col'), may hold values from 57 to 115, as said below
- tok_count: int32 [16, 2], P('section'), may hold values from 64 to 256, as said below
- owner_order: int32 [16, 64], P('section'), may hold values from 0 to 63, each once within a row
Outputs:
- y_next: bfloat16 [4096, 12288], P(('section', 'row', 'col'))
- dx_section: bfloat16 [4096, 12288], P(('section', 'row', 'col'))
Inputs may be any that keep to these rules, and one draw needn't show every extreme that they name: At each grid position the slots below blk_count name distinct block positions (blk_row, blk_col); the other slots name arbitrary positions. `blk_col`: see blk_row. `blk_count`: some grid position of every draw holds exactly 115 live slots. `tok_count`: index 0 counts the forward micro-batch, index 1 the backward one; valid tokens come first; some entry of every draw equals 256. `owner_order`: each section's row is a permutation.
All inputs are finite; a program needn't handle non-finite values.
Results may differ from a plain program's by a relative error of at most 0.015.
Values may be sent and summed in bfloat16 or wider, within the bound.
A program may use at most 128 MiB of HBM per device.

v0:
```python
import jax
import jax.numpy as jnp
from jax import lax
from jax.sharding import PartitionSpec as P


def passed_along(shard, axis, by):
    length = lax.axis_size(axis)
    pairs = [(i, i + by) for i in range(length) if 0 <= i + by < length]
    return lax.ppermute(shard, axis, pairs)


def local(x_fwd, dy_bwd, w_blocks, blk_row, blk_col, blk_count, tok_count, owner_order):
    row_count = lax.axis_size("row")
    col_count = lax.axis_size("col")
    token_total, in_width = x_fwd.shape
    out_width = dy_bwd.shape[1]
    slot_total = w_blocks.shape[3]
    block_size = w_blocks.shape[5]
    block_rows = in_width // block_size
    block_cols = out_width // block_size
    owned_rows = token_total // (row_count * col_count)
    weights = w_blocks.reshape(slot_total, block_size, block_size)
    live = (jnp.arange(slot_total) < blk_count.reshape(())).astype(weights.dtype)
    dense_blocks = jnp.zeros((block_rows, block_cols, block_size, block_size), weights.dtype)
    dense_blocks = dense_blocks.at[blk_row.reshape(slot_total), blk_col.reshape(slot_total)].add(
        weights * live[:, None, None]
    )
    dense_weight = jnp.transpose(dense_blocks, (0, 2, 1, 3)).reshape(in_width, out_width)
    limits = tok_count.reshape(2)
    block_total = owner_order.shape[1]
    block_length = token_total // block_total
    token_index = (
        owner_order.reshape(block_total)[:, None] * block_length + jnp.arange(block_length)[None, :]
    ).reshape(token_total)
    ordered_rows = jnp.take(x_fwd, token_index, axis=0)
    ordered_rows = jnp.where(
        (token_index < limits[0])[:, None], ordered_rows, jnp.zeros_like(ordered_rows)
    )
    partial_value = jnp.dot(ordered_rows, dense_weight, preferred_element_type=jnp.float32).astype(
        jnp.bfloat16
    )
    outgoing = partial_value.reshape(row_count * col_count, owned_rows, out_width)
    received = lax.all_to_all(outgoing, ("row", "col"), split_axis=0, concat_axis=2, tiled=True)
    summed = received.reshape(owned_rows, row_count, col_count * out_width).astype(jnp.float32)
    forward_act = jnp.sum(summed, axis=1).astype(jnp.bfloat16)
    y_next = passed_along(forward_act, "section", 1)
    grad_rows = dy_bwd.shape[0]
    grad_index = lax.axis_index("row") * grad_rows + jnp.arange(grad_rows)
    grad_kept = jnp.where((grad_index < limits[1])[:, None], dy_bwd, jnp.zeros_like(dy_bwd))
    grad_partial = lax.dot_general(
        lax.all_gather(grad_kept, "row", axis=0, tiled=True),
        dense_weight,
        (((1,), (1,)), ((), ())),
        preferred_element_type=jnp.float32,
    ).astype(jnp.bfloat16)
    grad_outgoing = grad_partial.reshape(row_count * col_count, owned_rows, in_width)
    grad_received = lax.all_to_all(
        grad_outgoing, ("row", "col"), split_axis=0, concat_axis=2, tiled=True
    )
    grad_summed = grad_received.reshape(owned_rows, row_count, col_count, in_width).astype(
        jnp.float32
    )
    dx_section = (
        jnp.sum(grad_summed, axis=2).reshape(owned_rows, row_count * in_width).astype(jnp.bfloat16)
    )
    return (y_next, dx_section)


def solution(mesh):
    return jax.shard_map(
        local,
        mesh=mesh,
        in_specs=(
            P("section", "row"),
            P(("section", "row"), "col"),
            P("section", "row", "col", None, None, None),
            P("section", "row", "col", None),
            P("section", "row", "col", None),
            P("section", "row", "col"),
            P("section", None),
            P("section", None),
        ),
        out_specs=(P(("section", "row", "col"), None), P(("section", "row", "col"), None)),
        check_vma=False,
    )
```

profile of v0, /device:TPU:1, one launch (start us, length us, event | category | flops | bytes accessed | tf_op | source)
XLA Modules:
  0.0 134.2 jit_solution(12094650554060465217)
XLA Ops:
  7.2 0.0 copy-start
  7.2 0.0 all-gather.2.cloned.1.call-start
  7.2 1.3 fusion.28
  8.5 0.7 add_compare_fusion
  9.2 1.7 %broadcast_select_fusion = bf16[32,3072]{1,0:T(8,128)(2,1)} fusion(bf16[32,3072]{1,0:T(8,128)(2,1)} %param.9, pred[32]{0:T(512)(128)(4,1)S(1)} %add_compare_fusion), kind=kLoop, calls=%fused_computation.20 | loop fusion | flops 98304 | bytes 393248 | tf_op jit(solution)/shard_map/jit(_where)/select_n | solution.py:50
  10.9 0.0 all-gather.2.cloned.1.call-update
  11.6 0.7 multiply_bitcast_fusion
  12.2 0.1 iota_add_fusion
  12.3 0.1 add.97
  12.4 0.1 add.94
  12.5 0.7 fusion.25
  13.2 4.2 %bitcast_multiply_fusion = bf16[115,128,128]{2,1,0:T(8,128)(2,1)} fusion(bf16[1,1,1,115,128,128]{5,4,3,2,1,0:T(8,128)(2,1)} %param.10, bf16[115]{0:T(256)(128)(2,1)S(1)} %compare_convert_fusion), kind=kLoop, calls=%fused_computation.9 | loop fusion | flops 1884160 | bytes 7536870 | tf_op jit(solution)/shard_map/mul | solution.py:27
  17.4 6.0 %broadcast_in_dim.45 = bf16[12,24,128,128]{3,2,1,0:T(8,128)(2,1)} broadcast(bf16[]{:T(256)} %constant.9.clone.1), dimensions={} | broadcast | bytes 9437186 | tf_op jit(solution)/shard_map/broadcast_in_dim | solution.py:25
  23.4 27.2 %scatter_fusion = bf16[12,24,128,128]{3,2,1,0:T(8,128)(2,1)} fusion(bf16[12,24,128,128]{3,2,1,0:T(8,128)(2,1)} %broadcast_in_dim.45, s32[115]{0:T(128)S(1)} %fusion.25, bf16[115,128,128]{2,1,0:T(8,128)(2,1)} %bitcast_multiply_fusion), kind=kCustom, calls=%fused_computation.1 | custom fusion | flops 1884160 | bytes 11305880 | tf_op jit(solution)/shard_map/scatter-add | solution.py:26
  50.6 14.6 %copy.13 = bf16[12,128,24,128]{3,2,1,0:T(8,128)(2,1)} copy(bf16[12,128,24,128]{3,1,2,0:T(8,128)(2,1)} %bitcast.52) | data formatting | bytes 18874368 | tf_op jit(solution)/shard_map/transpose | solution.py:29
  65.2 0.0 copy-done
  65.3 1.3 gather_fusion
  66.5 0.6 broadcast_compare_fusion
  67.2 7.5 %fusion.9 = bf16[32,8,3072]{2,1,0:T(8,128)(2,1)} fusion(bf16[192,8,24,128]{3,2,1,0:T(8,128)(2,1)} %bitcast.53, bf16[256,1536]{1,0:T(8,128)(2,1)S(1)} %gather_fusion, pred[256]{0:T(512)(128)(4,1)S(1)} %get-tuple-element.3, pred[256]{0:T(512)(128)(4,1)S(1)} %get-tuple-element.2), kind=kOutput, calls=%fused_computation.10 | convolution fusion | flops 2417491968 | bytes 11796992 | tf_op jit(solution)/shard_map/dot_general | solution.py:40
  74.7 10.5 %all-to-all-start = ((bf16[32,8,3072]{2,1,0:T(8,128)(2,1)}), bf16[32,8,3072]{2,1,0:T(8,128)(2,1)S(1)}, u32[]{:S(2)}, u32[]{:S(2)}) async-start(bf16[32,8,3072]{2,1,0:T(8,128)(2,1)} %fusion.9), calls=%async_computation | async-start | bytes 3145728 | tf_op jit(solution)/shard_map/all_to_all | solution.py:44
  85.3 0.0 all-gather.2.cloned.1.call-done
  85.3 7.7 %fusion.15 = bf16[32,8,1536]{2,1,0:T(8,128)(2,1)} fusion(bf16[256,3072]{1,0:T(8,128)(2,1)} %all-gather.2.cloned.1.call-done, bf16[192,8,24,128]{3,2,1,0:T(8,128)(2,1)} %bitcast.54), kind=kOutput, calls=%fused_computation.12 | convolution fusion | flops 2416312320 | bytes 11796480 | tf_op jit(solution)/shard_map/dot_general | solution.py:51
  93.0 13.7 %all-to-all-done = bf16[32,8,3072]{2,1,0:T(8,128)(2,1)S(1)} async-done(((bf16[32,8,3072]{2,1,0:T(8,128)(2,1)}), bf16[32,8,3072]{2,1,0:T(8,128)(2,1)S(1)}, u32[]{:S(2)}, u32[]{:S(2)}) %all-to-all-start) | async-done | bytes 1572896 | tf_op jit(solution)/shard_map/all_to_all | solution.py:44
  106.7 5.6 %all-to-all-start.1 = ((bf16[32,8,1536]{2,1,0:T(8,128)(2,1)}), bf16[32,8,1536]{2,1,0:T(8,128)(2,1)S(1)}, u32[]{:S(2)}, u32[]{:S(2)}) async-start(bf16[32,8,1536]{2,1,0:T(8,128)(2,1)} %fusion.15), calls=%async_computation.1 | async-start | bytes 1572864 | tf_op jit(solution)/shard_map/all_to_all | solution.py:58
  112.3 2.0 %copy.14 = bf16[1,8,32,3072]{3,2,1,0:T(8,128)(2,1)} copy(bf16[1,8,32,3072]{3,1,2,0:T(8,128)(2,1)S(1)} %bitcast.55) | data formatting | bytes 3145728 | tf_op jit(solution)/shard_map/all_to_all | solution.py:44
  114.3 2.9 %reshape.169 = bf16[8,8,12288]{2,1,0:T(8,128)(2,1)S(1)} reshape(bf16[1,8,32,3072]{3,2,1,0:T(8,128)(2,1)} %copy.14) | data formatting | bytes 3145728 | tf_op jit(solution)/shard_map/reshape | solution.py:45
  117.2 1.0 reduce_sum.21
  118.3 1.5 %collective-permute-start = (bf16[8,12288]{1,0:T(8,128)(2,1)S(1)}, bf16[8,12288]{1,0:T(8,128)(2,1)S(1)}, u32[]{:S(2)}, u32[]{:S(2)}) collective-permute-start(bf16[8,12288]{1,0:T(8,128)(2,1)S(1)} %reduce_sum.21), channel_id=1, source_target_pairs={{0,32},{32,64},{64,96},{96,128},{128,160},{160,192},{192,224},{224... | collective-permute-start | bytes 589832 | tf_op jit(solution)/shard_map/ppermute | solution.py:10
  119.8 4.0 %collective-permute-done = bf16[8,12288]{1,0:T(8,128)(2,1)S(1)} collective-permute-done((bf16[8,12288]{1,0:T(8,128)(2,1)S(1)}, bf16[8,12288]{1,0:T(8,128)(2,1)S(1)}, u32[]{:S(2)}, u32[]{:S(2)}) %collective-permute-start) | collective-permute-done | bytes 196640 | tf_op jit(solution)/shard_map/ppermute | solution.py:10
  123.8 2.1 %all-to-all-done.1 = bf16[32,8,1536]{2,1,0:T(8,128)(2,1)S(1)} async-done(((bf16[32,8,1536]{2,1,0:T(8,128)(2,1)}), bf16[32,8,1536]{2,1,0:T(8,128)(2,1)S(1)}, u32[]{:S(2)}, u32[]{:S(2)}) %all-to-all-start.1) | async-done | bytes 786464 | tf_op jit(solution)/shard_map/all_to_all | solution.py:58
  125.9 0.8 bitcast_reduce_fusion
  126.7 0.7 copy.35
  (3 shorter events, 0.0 us)
Async XLA Ops:
  7.2 58.1 %copy-start = (bf16[256,1536]{1,0:T(8,128)(2,1)S(1)}, bf16[256,1536]{1,0:T(8,128)(2,1)}, u32[]{:S(2)}) copy-start(bf16[256,1536]{1,0:T(8,128)(2,1)} %param.8) | copy-start | bytes 2359300
  7.2 78.1 %all-gather.2.cloned.1.call-start = ((), (), s32[]{:S(2)}) async-start(), calls=%async_computation.2 | async-start | bytes 1769472 | tf_op jit(solution)/shard_map/all_gather | solution.py:52
  74.7 32.0 %all-to-all-start = ((bf16[32,8,3072]{2,1,0:T(8,128)(2,1)}), bf16[32,8,3072]{2,1,0:T(8,128)(2,1)S(1)}, u32[]{:S(2)}, u32[]{:S(2)}) async-start(bf16[32,8,3072]{2,1,0:T(8,128)(2,1)} %fusion.9), calls=%async_computation | async-start | bytes 3145728 | tf_op jit(solution)/shard_map/all_to_all | solution.py:44
  106.7 19.2 %all-to-all-start.1 = ((bf16[32,8,1536]{2,1,0:T(8,128)(2,1)}), bf16[32,8,1536]{2,1,0:T(8,128)(2,1)S(1)}, u32[]{:S(2)}, u32[]{:S(2)}) async-start(bf16[32,8,1536]{2,1,0:T(8,128)(2,1)} %fusion.15), calls=%async_computation.1 | async-start | bytes 1572864 | tf_op jit(solution)/shard_map/all_to_all | solution.py:58
  118.3 5.6 %collective-permute-start = (bf16[8,12288]{1,0:T(8,128)(2,1)S(1)}, bf16[8,12288]{1,0:T(8,128)(2,1)S(1)}, u32[]{:S(2)}, u32[]{:S(2)}) collective-permute-start(bf16[8,12288]{1,0:T(8,128)(2,1)S(1)} %reduce_sum.21), channel_id=1, source_target_pairs={{0,32},{32,64},{64,96},{96,128},{128,160},{160,192},{192,224},{224... | collective-permute-start | bytes 589832 | tf_op jit(solution)/shard_map/ppermute | solution.py:10
Sparse Core Ops, SparseCore 0:
  11.0 37.7 all-gather.1
where the time goes:
time: 135 us; the launch traced here: 134 us
  other arithmetic  37.6 us (28%)
  local copies, waits for them, and re-layouts  29.1 us (22%)
  waiting for transfers between devices  19.9 us (15%)
  starting transfers between devices  17.7 us (13%)
  matrix products  15.2 us (11%)
  between operations  14.8 us (11%)
    scatter-add x1, other arithmetic, local(): dense_blocks.at[blk_row.reshape(slot_total), blk_col.reshape(slot_total)]  27.2 us
    transpose x1, local copies, waits for them, and re-layouts, local(): jnp.transpose(dense_blocks, (0, 2, 1, 3)).reshape(in_width, out_width)  14.6 us
    all_to_all x1, waiting for transfers between devices, local(): lax.all_to_all(outgoing, ('row', 'col'), split_axis=0, concat_axis=2, til...  13.7 us
    all_to_all x1, starting transfers between devices, local(): lax.all_to_all(outgoing, ('row', 'col'), split_axis=0, concat_axis=2, til...  10.5 us
    dot_general x1, matrix products, local(): lax.dot_general(lax.all_gather(grad_kept, 'row', axis=0, tiled=True), den...  7.69 us
    dot_general x1, matrix products, local(): jnp.dot(ordered_rows, dense_weight, preferred_element_type=jnp.float32)  7.55 us
    broadcast_in_dim x1, local copies, waits for them, and re-layouts, local(): jnp.zeros((block_rows, block_cols, block_size, block_size), weights.dtype)  6.03 us
    all_to_all x1, starting transfers between devices, local(): lax.all_to_all(grad_outgoing, ('row', 'col'), split_axis=0, concat_axis=2...  5.56 us
  transfers between devices with their start and end apart: 4, of which 3 were waited for; matrix products, arithmetic and copies ran while one was open for 57% of the time, Pallas kernels for 0%

commit v1 on v0

--- a/solution.py
+++ b/solution.py
@@ -2,6 +2,14 @@
 import jax.numpy as jnp
 from jax import lax
 from jax.sharding import PartitionSpec as P
+from jax.lax import all_to_all, axis_size
+
+take_the_clusters = lambda x_in: jnp.concatenate(
+    all_to_all(
+        jnp.stack(jnp.split(x_in, axis_size(("row", "col")), axis=0), axis=0), ("row", "col"), 0, 0
+    ),
+    2,
+)
 
 
 def passed_along(shard, axis, by):
@@ -41,7 +49,7 @@
         jnp.bfloat16
     )
     outgoing = partial_value.reshape(row_count * col_count, owned_rows, out_width)
-    received = lax.all_to_all(outgoing, ("row", "col"), split_axis=0, concat_axis=2, tiled=True)
+    received = take_the_clusters(outgoing)
     summed = received.reshape(owned_rows, row_count, col_count * out_width).astype(jnp.float32)
     forward_act = jnp.sum(summed, axis=1).astype(jnp.bfloat16)
     y_next = passed_along(forward_act, "section", 1)

time: 135 us -> 154 us (1.14)
  local copies, waits for them, and re-layouts: 29.1 us -> 48.9 us
    unnamed x3 -> x34, local copies, waits for them, and re-layouts: 0.69 us -> 19.9 us
    another operation x0 -> x2, local copies, waits for them, and re-layouts: none -> 3.51 us  [the longest x1 2.89 us: local(): received.reshape(owned_rows, row_count, col_count * out_width)]
    all_to_all x1 -> x0, local copies, waits for them, and re-layouts: 2.04 us -> none  [local(): lax.all_to_all(outgoing, ('row', 'col'), split_axis=0, concat_axis=2, til...]
  transfers between devices with their start and end apart: 4 -> 4, of which waited for: 3 -> 3; matrix products, arithmetic and copies ran while one was open for 57% -> 62% of each run, Pallas kernels for 0% -> 0%
where the time goes in v1:
time: 154 us; the launch traced here: 153 us
  local copies, waits for them, and re-layouts  48.9 us (32%)
  other arithmetic  37.6 us (24%)
  waiting for transfers between devices  19.9 us (13%)
  starting transfers between devices  17.7 us (11%)
  between operations  14.8 us (10%)
  matrix products  14.1 us (9%)
    scatter-add x1, other arithmetic, local(): dense_blocks.at[blk_row.reshape(slot_total), blk_col.reshape(slot_total)]  27.2 us
    unnamed x34, local copies, waits for them, and re-layouts  19.9 us
    transpose x1, local copies, waits for them, and re-layouts, local(): jnp.transpose(dense_blocks, (0, 2, 1, 3)).reshape(in_width, out_width)  14.6 us
    all_to_all x1, waiting for transfers between devices, all_to_all(jnp.stack(jnp.split(x_in, axis_size(('row', 'col')), axis=0),...  13.7 us
    all_to_all x1, starting transfers between devices, all_to_all(jnp.stack(jnp.split(x_in, axis_size(('row', 'col')), axis=0),...  10.5 us
    dot_general x1, matrix products, local(): lax.dot_general(lax.all_gather(grad_kept, 'row', axis=0, tiled=True), den...  7.69 us
    dot_general x1, matrix products, local(): jnp.dot(ordered_rows, dense_weight, preferred_element_type=jnp.float32)  6.37 us
    broadcast_in_dim x1, local copies, waits for them, and re-layouts, local(): jnp.zeros((block_rows, block_cols, block_size, block_size), weights.dtype)  6.03 us
  transfers between devices with their start and end apart: 4, of which 3 were waited for; matrix products, arithmetic and copies ran while one was open for 62% of the time, Pallas kernels for 0%

profile of v1, /device:TPU:1, one launch (start us, length us, event | category | flops | bytes accessed | tf_op | source)
XLA Modules:
  0.0 152.9 jit_solution(10597015855336337134)
XLA Ops:
  7.2 1.3 fusion.25
  8.5 0.7 add_compare_fusion
  9.2 1.7 %broadcast_select_fusion = bf16[32,3072]{1,0:T(8,128)(2,1)} fusion(bf16[32,3072]{1,0:T(8,128)(2,1)} %param.9, pred[32]{0:T(512)(128)(4,1)S(1)} %add_compare_fusion), kind=kLoop, calls=%fused_computation.19 | loop fusion | flops 98304 | bytes 393248 | tf_op jit(solution)/shard_map/jit(_where)/select_n | solution.py:58
  10.9 0.7 multiply_bitcast_fusion
  12.5 0.7 fusion.22
  13.2 4.2 %bitcast_multiply_fusion = bf16[115,128,128]{2,1,0:T(8,128)(2,1)} fusion(bf16[1,1,1,115,128,128]{5,4,3,2,1,0:T(8,128)(2,1)} %param.10, bf16[115]{0:T(256)(128)(2,1)S(1)} %compare_convert_fusion), kind=kLoop, calls=%fused_computation.9 | loop fusion | flops 1884160 | bytes 7536870 | tf_op jit(solution)/shard_map/mul | solution.py:35
  17.4 6.0 %broadcast_in_dim.45 = bf16[12,24,128,128]{3,2,1,0:T(8,128)(2,1)} broadcast(bf16[]{:T(256)} %constant.9.clone.1), dimensions={} | broadcast | bytes 9437186 | tf_op jit(solution)/shard_map/broadcast_in_dim | solution.py:33
  23.5 27.2 %scatter_fusion = bf16[12,24,128,128]{3,2,1,0:T(8,128)(2,1)} fusion(bf16[12,24,128,128]{3,2,1,0:T(8,128)(2,1)} %broadcast_in_dim.45, s32[115]{0:T(128)S(1)} %fusion.22, bf16[115,128,128]{2,1,0:T(8,128)(2,1)} %bitcast_multiply_fusion), kind=kCustom, calls=%fused_computation.1 | custom fusion | flops 1884160 | bytes 11305880 | tf_op jit(solution)/shard_map/scatter-add | solution.py:34
  50.6 14.6 %copy.11 = bf16[12,128,24,128]{3,2,1,0:T(8,128)(2,1)} copy(bf16[12,128,24,128]{3,1,2,0:T(8,128)(2,1)} %bitcast.174) | data formatting | bytes 18874368 | tf_op jit(solution)/shard_map/transpose | solution.py:37
  65.3 1.3 gather_fusion
  66.5 0.6 broadcast_compare_fusion
  67.2 6.4 %fusion.6 = bf16[256,3072]{1,0:T(8,128)(2,1)S(1)} fusion(bf16[192,8,24,128]{3,2,1,0:T(8,128)(2,1)} %bitcast.175, bf16[256,1536]{1,0:T(8,128)(2,1)S(1)} %gather_fusion, pred[256]{0:T(512)(128)(4,1)S(1)} %get-tuple-element.3, pred[256]{0:T(512)(128)(4,1)S(1)} %get-tuple-element.2), kind=kOutput, calls=%fused_computation.8 | convolution fusion | flops 2417491968 | bytes 11796992 | tf_op jit(solution)/shard_map/dot_general | solution.py:48
  74.2 0.6 constant_dynamic-update-slice_fusion.30
  76.6 0.6 constant_dynamic-update-slice_fusion.26
  83.5 0.6 constant_dynamic-update-slice_fusion.15
  84.1 0.6 constant_dynamic-update-slice_fusion.14
  85.9 0.6 constant_dynamic-update-slice_fusion.11
  87.8 0.6 constant_dynamic-update-slice_fusion.8
  90.9 0.6 constant_dynamic-update-slice_fusion.3
  91.5 0.6 constant_dynamic-update-slice_fusion.2
  93.4 10.5 %all-to-all-start = ((bf16[32,1,8,3072]{3,2,1,0:T(8,128)(2,1)}), bf16[32,1,8,3072]{3,2,1,0:T(8,128)(2,1)S(1)}, u32[]{:S(2)}, u32[]{:S(2)}) async-start(bf16[32,1,8,3072]{3,2,1,0:T(8,128)(2,1)} %constant_dynamic-update-slice_fusion), calls=%async_computation | async-start | bytes 3145728 | tf_op jit(solution)/shard_map/all_to_all | solution.py:8
  104.0 7.7 %fusion.12 = bf16[32,8,1536]{2,1,0:T(8,128)(2,1)} fusion(bf16[256,3072]{1,0:T(8,128)(2,1)} %all-gather.2.cloned.1.call-done, bf16[192,8,24,128]{3,2,1,0:T(8,128)(2,1)} %bitcast.176), kind=kOutput, calls=%fused_computation.11 | convolution fusion | flops 2416312320 | bytes 11796480 | tf_op jit(solution)/shard_map/dot_general | solution.py:59
  111.7 13.7 %all-to-all-done = bf16[32,1,8,3072]{3,2,1,0:T(8,128)(2,1)S(1)} async-done(((bf16[32,1,8,3072]{3,2,1,0:T(8,128)(2,1)}), bf16[32,1,8,3072]{3,2,1,0:T(8,128)(2,1)S(1)}, u32[]{:S(2)}, u32[]{:S(2)}) %all-to-all-start) | async-done | bytes 1572896 | tf_op jit(solution)/shard_map/all_to_all | solution.py:8
  125.4 5.6 %all-to-all-start.1 = ((bf16[32,8,1536]{2,1,0:T(8,128)(2,1)}), bf16[32,8,1536]{2,1,0:T(8,128)(2,1)S(1)}, u32[]{:S(2)}, u32[]{:S(2)}) async-start(bf16[32,8,1536]{2,1,0:T(8,128)(2,1)} %fusion.12), calls=%async_computation.1 | async-start | bytes 1572864 | tf_op jit(solution)/shard_map/all_to_all | solution.py:66
  130.9 2.0 %copy.12 = bf16[1,8,32,3072]{3,2,1,0:T(8,128)(2,1)} copy(bf16[1,8,32,3072]{3,1,0,2:T(8,128)(2,1)S(1)} %bitcast.177) | data formatting | bytes 3145728 | tf_op jit(solution)/shard_map/reshape | solution.py:7
  133.0 2.9 %reshape_reshape.3 = bf16[8,8,12288]{2,1,0:T(8,128)(2,1)S(1)} reshape(bf16[1,8,32,3072]{3,2,1,0:T(8,128)(2,1)} %copy.12) | data formatting | bytes 3145728 | tf_op jit(solution)/shard_map/reshape;reshape | solution.py:53
  135.9 1.0 reduce_sum.21
  136.9 1.5 %collective-permute-start = (bf16[8,12288]{1,0:T(8,128)(2,1)S(1)}, bf16[8,12288]{1,0:T(8,128)(2,1)S(1)}, u32[]{:S(2)}, u32[]{:S(2)}) collective-permute-start(bf16[8,12288]{1,0:T(8,128)(2,1)S(1)} %reduce_sum.21), channel_id=1, source_target_pairs={{0,32},{32,64},{64,96},{96,128},{128,160},{160,192},{192,224},{224... | collective-permute-start | bytes 589832 | tf_op jit(solution)/shard_map/ppermute | solution.py:18
  138.5 4.0 %collective-permute-done = bf16[8,12288]{1,0:T(8,128)(2,1)S(1)} collective-permute-done((bf16[8,12288]{1,0:T(8,128)(2,1)S(1)}, bf16[8,12288]{1,0:T(8,128)(2,1)S(1)}, u32[]{:S(2)}, u32[]{:S(2)}) %collective-permute-start) | collective-permute-done | bytes 196640 | tf_op jit(solution)/shard_map/ppermute | solution.py:18
  142.5 2.1 %all-to-all-done.1 = bf16[32,8,1536]{2,1,0:T(8,128)(2,1)S(1)} async-done(((bf16[32,8,1536]{2,1,0:T(8,128)(2,1)}), bf16[32,8,1536]{2,1,0:T(8,128)(2,1)S(1)}, u32[]{:S(2)}, u32[]{:S(2)}) %all-to-all-start.1) | async-done | bytes 786464 | tf_op jit(solution)/shard_map/all_to_all | solution.py:66
  144.6 0.8 bitcast_reduce_fusion
  145.4 0.7 copy.62
  (35 shorter events, 15.2 us)
Async XLA Ops:
  7.2 58.1 %copy-start = (bf16[256,1536]{1,0:T(8,128)(2,1)S(1)}, bf16[256,1536]{1,0:T(8,128)(2,1)}, u32[]{:S(2)}) copy-start(bf16[256,1536]{1,0:T(8,128)(2,1)} %param.8) | copy-start | bytes 2359300
  7.2 96.8 %all-gather.2.cloned.1.call-start = ((), (), s32[]{:S(2)}) async-start(), calls=%async_computation.2 | async-start | bytes 1769472 | tf_op jit(solution)/shard_map/all_gather | solution.py:60
  93.4 32.0 %all-to-all-start = ((bf16[32,1,8,3072]{3,2,1,0:T(8,128)(2,1)}), bf16[32,1,8,3072]{3,2,1,0:T(8,128)(2,1)S(1)}, u32[]{:S(2)}, u32[]{:S(2)}) async-start(bf16[32,1,8,3072]{3,2,1,0:T(8,128)(2,1)} %constant_dynamic-update-slice_fusion), calls=%async_computation | async-start | bytes 3145728 | tf_op jit(solution)/shard_map/all_to_all | solution.py:8
  125.4 19.2 %all-to-all-start.1 = ((bf16[32,8,1536]{2,1,0:T(8,128)(2,1)}), bf16[32,8,1536]{2,1,0:T(8,128)(2,1)S(1)}, u32[]{:S(2)}, u32[]{:S(2)}) async-start(bf16[32,8,1536]{2,1,0:T(8,128)(2,1)} %fusion.12), calls=%async_computation.1 | async-start | bytes 1572864 | tf_op jit(solution)/shard_map/all_to_all | solution.py:66
  136.9 5.6 %collective-permute-start = (bf16[8,12288]{1,0:T(8,128)(2,1)S(1)}, bf16[8,12288]{1,0:T(8,128)(2,1)S(1)}, u32[]{:S(2)}, u32[]{:S(2)}) collective-permute-start(bf16[8,12288]{1,0:T(8,128)(2,1)S(1)} %reduce_sum.21), channel_id=1, source_target_pairs={{0,32},{32,64},{64,96},{96,128},{128,160},{160,192},{192,224},{224... | collective-permute-start | bytes 589832 | tf_op jit(solution)/shard_map/ppermute | solution.py:18
Sparse Core Ops, SparseCore 0:
  11.0 37.7 all-gather.1
